TPU v7x, 256 devices: a whole 4x4x8 slice. The times are simulated.
256 devices in a mesh: section: 2 (over z_lo), seq: 32 (over x, z_hi, core), tp: 4 (over y).
Axes of the slice: x: 4, y: 4, z: 8 (z_hi: 4, z_lo: 2; z = z_hi * 2 + z_lo), core: 2. Of those that a mesh axis runs over, the one named last changes fastest.
Arguments:
- hidden: bfloat16 [1024, 3072], P('seq', 'tp'), may hold values from -6 to 6
- qkv_weight: bfloat16 [2, 3072, 3, 1536], P('section', None, None, 'tp'), may hold values from -0.109375 to 0.109375
- qk_gain: float32 [2, 2, 64], P('section'), may hold values from 1.3 to 2
- out_weight: bfloat16 [2, 1536, 3072], P('section', 'tp'), may hold values from -0.15625 to 0.15625
- mod_weight: bfloat16 [2, 512, 18432], P('section', None, ('seq', 'tp')), may hold values from -0.5 to 0.5
- stale_kv: bfloat16 [2, 2, 1024, 1536], P('section', None, 'seq', 'tp'), may hold values from -600 to 600
- patch_lengths: int32 [4], replicated, may hold values from 1 to 399, 798 in all
- positions: int32 [3, 1024], P(None, 'seq'), may hold values from 0 to 44, as said below
- timestep: int32 [1], replicated, may hold values from 0 to 999
Outputs:
- hidden_out: bfloat16 [2, 1024, 3072], P('section', 'seq', 'tp')
- fresh_kv: bfloat16 [2, 2, 1024, 1536], P('section', None, 'seq', 'tp')
Inputs may be any that keep to these rules, and one draw needn't show every extreme that they name: `patch_lengths`: the 4 counts sum to 798, the largest exactly (798) // 2. `positions`: frames lie below 13, rows below 30, columns below 45.
All inputs are finite; a program needn't handle non-finite values.
Results may differ from a plain program's by a relative error of at most 0.025.
Values may be sent and summed in bfloat16 or wider, within the bound.
A program may use at most 64 MiB of HBM per device.

v0:
```python
import math
import jax
import jax.numpy as jnp
from jax import lax
from jax.sharding import PartitionSpec as P

HEAD = 64
TEMB = 512
TEXT = 226


def shifted(value, axis, steps):
    count = lax.axis_size(axis)
    first, last = (max(0, -steps), min(count, count - steps))
    return lax.ppermute(value, axis, [(source, source + steps) for source in range(first, last)])


def patch_index(index, bounds):
    video_row = index - TEXT
    patch_id = jnp.sum((video_row[:, None] >= bounds[None, :-1]).astype(jnp.int32), axis=1)
    return jnp.where(index < TEXT, 0, patch_id)


def time_features(timestep):
    half_width = TEMB // 2
    frequency = jnp.exp(
        -math.log(10000.0) * jnp.arange(half_width).astype(jnp.float32) / half_width
    )
    phases = timestep.astype(jnp.float32)[:, None] * frequency[None, :]
    embedded = jnp.concatenate([jnp.cos(phases), jnp.sin(phases)], axis=1)
    return jax.nn.silu(embedded).astype(jnp.bfloat16)


def axis_freq(dim_size):
    return 1.0 / 10000.0 ** (jnp.arange(0, dim_size, 2).astype(jnp.float32) / dim_size)


def rope_tables(positions, head_count):
    coords = positions.astype(jnp.float32)
    angles = jnp.concatenate(
        [
            coords[0][:, None] * axis_freq(HEAD // 4)[None, :],
            coords[1][:, None] * axis_freq(3 * HEAD // 8)[None, :],
            coords[2][:, None] * axis_freq(3 * HEAD // 8)[None, :],
        ],
        axis=1,
    )
    angles = jnp.repeat(angles, 2, axis=1)
    return (jnp.tile(jnp.cos(angles), (1, head_count)), jnp.tile(jnp.sin(angles), (1, head_count)))


def rotate_pairs(values):
    column = jnp.arange(values.shape[-1])
    return jnp.where(column % 2 == 0, -jnp.roll(values, -1, axis=-1), jnp.roll(values, 1, axis=-1))


def head_norm(values, gain):
    parts = values.reshape(values.shape[0], -1, HEAD)
    average = jnp.mean(parts, axis=-1, keepdims=True)
    centred = parts - average
    variance = jnp.mean(centred * centred, axis=-1, keepdims=True)
    return (centred * lax.rsqrt(variance + 1e-06) * gain).reshape(values.shape)


def merge_block(running, query_heads, query_patch, fresh_block, stale_block, bounds):
    highest, denominator, accumulated = running
    key_count = fresh_block.shape[1]
    head_count = query_heads.shape[1]
    key_rows = jnp.arange(key_count, dtype=jnp.int32)
    allowed = (patch_index(key_rows, bounds)[None, :] <= query_patch[:, None])[None]
    fresh_keys = fresh_block[0].reshape(key_count, head_count, HEAD)
    fresh_vals = fresh_block[1].reshape(key_count, head_count, HEAD)
    stale_keys = stale_block[0].reshape(key_count, head_count, HEAD)
    stale_vals = stale_block[1].reshape(key_count, head_count, HEAD)
    scores_fresh = jnp.einsum(
        "thd,rhd->htr", query_heads, fresh_keys, preferred_element_type=jnp.float32
    )
    scores_stale = jnp.einsum(
        "thd,rhd->htr", query_heads, stale_keys, preferred_element_type=jnp.float32
    )
    scores = jnp.where(allowed, scores_fresh, scores_stale) * HEAD ** (-0.5)
    new_high = jnp.maximum(highest, jnp.max(scores, axis=2))
    rescale = jnp.exp(highest - new_high)
    weights_soft = jnp.exp(scores - new_high[:, :, None])
    denominator = jnp.sum(weights_soft, axis=2)
    part_fresh = jnp.where(allowed, weights_soft, 0.0).astype(jnp.bfloat16)
    part_stale = jnp.where(allowed, 0.0, weights_soft).astype(jnp.bfloat16)
    accumulated = accumulated * rescale[:, :, None]
    accumulated = jnp.einsum(
        "htr,rhd->htd", part_fresh, fresh_vals, preferred_element_type=jnp.float32
    )
    accumulated = accumulated + jnp.einsum(
        "htr,rhd->htd", part_stale, stale_vals, preferred_element_type=jnp.float32
    )
    return (new_high, denominator, accumulated)


def local(
    hidden,
    qkv_weight,
    qk_gain,
    out_weight,
    mod_weight,
    stale_kv,
    patch_lengths,
    positions,
    timestep,
):
    tok_rows = hidden.shape[0]
    feat_share = hidden.shape[1]
    model_width = feat_share * lax.axis_size("tp")
    head_cols = qkv_weight.shape[3]
    head_count = head_cols // HEAD
    seq_rank = lax.axis_index("seq")
    tp_rank = lax.axis_index("tp")
    section_rank = lax.axis_index("section")
    mod_share = jnp.dot(time_features(timestep), mod_weight[0], preferred_element_type=jnp.float32)[
        0
    ]
    by_tp = lax.all_gather(mod_share[None, None, :], "tp", axis=0, tiled=True)
    modulate = lax.all_gather(
        jnp.pad(by_tp.reshape(1, 4, -1), ((0, 0), (0, 4), (0, 0))), "seq", axis=0, tiled=True
    )[:, :4].reshape(6, model_width)
    my_rows = seq_rank * tok_rows + jnp.arange(tok_rows, dtype=jnp.int32)
    video = (my_rows >= TEXT)[:, None]
    bounds = jnp.cumsum(patch_lengths)
    query_patch = patch_index(my_rows, bounds)
    cosine, sine_table = rope_tables(positions, head_count)
    shift_rows = jnp.where(video, modulate[0], modulate[3])
    scale_rows = jnp.where(video, modulate[1], modulate[4])
    gate_both = lax.dynamic_slice_in_dim(modulate, tp_rank * feat_share, feat_share, 1)
    gate_rows = jnp.where(video, gate_both[2], gate_both[5])
    weights_qkv = qkv_weight[0]
    gains = qk_gain[0]
    weights_out = out_weight[0]
    stale_own = stale_kv[0]

    def attend(queries, fresh_kv):
        query_heads = queries.reshape(tok_rows, head_count, HEAD)
        start_state = (
            jnp.full((head_count, tok_rows), -1e30, jnp.float32),
            jnp.zeros((head_count, tok_rows), jnp.float32),
            jnp.zeros((head_count, tok_rows, HEAD), jnp.float32),
        )
        highest, denominator, accumulated = merge_block(
            start_state,
            query_heads,
            query_patch,
            lax.all_gather(fresh_kv, "seq", axis=1, tiled=True),
            lax.all_gather(stale_own, "seq", axis=1, tiled=True),
            bounds,
        )
        blended = accumulated / denominator[:, :, None]
        return jnp.transpose(blended, (1, 0, 2)).reshape(tok_rows, head_cols).astype(jnp.bfloat16)

    def run_layer(incoming):
        features_all = lax.all_gather(incoming, "tp", axis=1, tiled=True).astype(jnp.float32)
        average = jnp.mean(features_all, axis=1, keepdims=True)
        centred = features_all - average
        variance = jnp.mean(centred * centred, axis=1, keepdims=True)
        normed = (centred * lax.rsqrt(variance + 1e-05) * (1.0 + scale_rows) + shift_rows).astype(
            jnp.bfloat16
        )
        proj = jnp.einsum("td,dcf->tcf", normed, weights_qkv, preferred_element_type=jnp.float32)
        queries = head_norm(proj[:, 0], gains[0])
        key_vecs = head_norm(proj[:, 1], gains[1])
        queries = jnp.where(
            video, queries * cosine + rotate_pairs(queries) * sine_table, queries
        ).astype(jnp.bfloat16)
        key_vecs = jnp.where(
            video, key_vecs * cosine + rotate_pairs(key_vecs) * sine_table, key_vecs
        ).astype(jnp.bfloat16)
        values = proj[:, 2].astype(jnp.bfloat16)
        fresh_kv = jnp.stack([key_vecs, values])
        attended = attend(queries, fresh_kv)
        projected = lax.psum_scatter(
            lax.dot_general(
                weights_out, attended, (((0,), (1,)), ((), ())), preferred_element_type=jnp.float32
            ).astype(jnp.bfloat16),
            "tp",
            scatter_dimension=0,
            tiled=True,
        ).astype(jnp.float32)
        result = (incoming.astype(jnp.float32) + gate_rows * projected.T).astype(jnp.bfloat16)
        return (result, fresh_kv)

    first_out, first_kv = run_layer(hidden)
    passed = shifted(first_out, "section", 1)
    second_out, second_kv = run_layer(passed)
    first_section = section_rank == 0
    hidden_out = jnp.where(first_section, first_out, second_out)[None]
    fresh_out = jnp.where(first_section, first_kv, second_kv)[None]
    return (hidden_out, fresh_out)


def solution(mesh):
    return jax.shard_map(
        local,
        mesh=mesh,
        in_specs=(
            P("seq", "tp"),
            P("section", None, None, "tp"),
            P("section", None, None),
            P("section", "tp", None),
            P("section", None, ("seq", "tp")),
            P("section", None, "seq", "tp"),
            P(),
            P(None, "seq"),
            P(),
        ),
        out_specs=(P("section", "seq", "tp"), P("section", None, "seq", "tp")),
        check_vma=False,
    )
```

profile of v0, /device:TPU:2, one launch (start us, length us, event | category | flops | bytes accessed | tf_op | source)
XLA Modules:
  0.0 375.8 jit_solution(1353841677514574803)
XLA Ops:
  11.3 10.7 %all-reduce.1 = f32[576]{0:T(1024)S(1)} all-reduce(f32[576]{0:T(1024)S(1)} %dynamic-update-slice), channel_id=2, replica_groups=mesh['section'=2,'seq'=32,'tp'=4] {'tp'}, use_global_device_ids=true, to_apply=%add.1 | all-reduce | flops 576 | bytes 4608
  22.1 42.5 %all_gather.23 = f32[32,8,144]{2,1,0:T(8,128)S(1)} all-gather(f32[1,8,144]{2,1,0:T(8,128)S(1)} %pad.4), channel_id=1, replica_groups=mesh['section'=2,'seq'=32,'tp'=4] {'seq'}, dimensions={0}, use_global_device_ids=true | all-gather | bytes 152064 | tf_op jit(solution)/shard_map/all_gather | solution.py:121
  64.9 12.3 %all_gather.24 = bf16[32,3072]{1,0:T(8,128)(2,1)S(1)} all-gather(bf16[32,768]{1,0:T(8,128)(2,1)} %param.9), channel_id=1, replica_groups=mesh['section'=2,'seq'=32,'tp'=4] {'tp'}, dimensions={1}, use_global_device_ids=true | all-gather | bytes 245760 | tf_op jit(solution)/shard_map/all_gather | solution.py:157
  77.6 4.4 %fusion.2 = f32[32,3,384]{2,0,1:T(8,128)S(1)} fusion(bf16[1,3072,3,384]{3,1,2,0:T(8,128)(2,1)} %param.10, bf16[32,3072]{1,0:T(8,128)(2,1)S(1)} %all_gather.24, f32[3072]{0:T(1024)S(1)} %bitcast.178, f32[3072]{0:T(1024)S(1)} %bitcast.180, f32[3072]{0:T(1024)S(1)} %bitcast.182, f32[3072]{0:T(1024)S(1)} %bitcast.176, f32[32]{0:T(128)S(1)} %add_rsqrt_fusion.5, ...), kind=kOutput, calls=%fused_computation.2 | convolution fusion | flops 227377152 | bytes 7471392 | tf_op jit(solution)/shard_map/td,dcf->tcf/dot_general | solution.py:164
  88.5 48.2 %all-gather.6.cloned.1.call-done = bf16[2,1024,384]{2,1,0:T(8,128)(2,1)} async-done(((bf16[2,32,384]{2,1,0:T(8,128)(2,1)}), bf16[2,1024,384]{2,1,0:T(8,128)(2,1)}) %all-gather.6.cloned.1.call-update) | async-done | bytes 1572880 | tf_op jit(solution)/shard_map/all_gather | solution.py:149
  136.7 2.4 fusion.128
  140.3 49.3 %all-gather.10.cloned.1.call-done = bf16[1,2,1024,384]{3,2,1,0:T(8,128)(2,1)} async-done(((bf16[1,2,32,384]{3,2,1,0:T(8,128)(2,1)}), bf16[1,2,1024,384]{3,2,1,0:T(8,128)(2,1)}) %all-gather.10.cloned.1.call-update) | async-done | bytes 1572880 | tf_op jit(solution)/shard_map/all_gather | solution.py:150
  189.6 2.7 fusion.127
  196.3 2.3 copy.167
  200.0 2.4 fusion.28
  202.4 2.3 copy.168
  204.7 1.8 fusion.15
  208.0 21.3 %reduce-scatter.3.cloned.1.call-done = bf16[768,32]{0,1:T(8,128)(2,1)} async-done(((bf16[3072,32]{0,1:T(8,128)(2,1)}), bf16[768,32]{0,1:T(8,128)(2,1)}) %reduce-scatter.3.cloned.1.call-update) | async-done | bytes 49168 | tf_op jit(solution)/shard_map/reduce_scatter | solution.py:176
  230.2 3.5 collective-permute-start
  233.6 1.7 collective-permute-done
  236.0 12.1 %all_gather.27 = bf16[32,3072]{1,0:T(8,128)(2,1)S(1)} all-gather(bf16[32,768]{1,0:T(8,128)(2,1)S(1)} %collective-permute-done), channel_id=1, replica_groups=mesh['section'=2,'seq'=32,'tp'=4] {'tp'}, dimensions={1}, use_global_device_ids=true | all-gather | bytes 245760 | tf_op jit(solution)/shard_map/all_gather | solution.py:157
  248.5 4.4 %fusion = f32[32,3,384]{2,0,1:T(8,128)S(1)} fusion(bf16[1,3072,3,384]{3,1,2,0:T(8,128)(2,1)} %param.10, bf16[32,3072]{1,0:T(8,128)(2,1)S(1)} %all_gather.27, f32[32]{0:T(128)S(1)} %add_rsqrt_fusion.4, f32[32]{0:T(128)S(1)} %broadcast_multiply_fusion.7, f32[3072]{0:T(1024)S(1)} %bitcast.179, f32[3072]{0:T(1024)S(1)} %bitcast.181, f32[3072]{0:T(1024)S(1)} %bitcast.183, ...), kind=kOutput, calls=%fused_computation | convolution fusion | flops 227377152 | bytes 7471392 | tf_op jit(solution)/shard_map/td,dcf->tcf/dot_general | solution.py:164
  264.4 1.6 mul.479
  266.0 1.5 sub.161.clone
  267.4 1.6 sub.163
  269.0 1.5 sub.165
  270.5 1.6 sub.169
  272.1 1.5 fusion.93
  284.1 1.5 fusion.71
  285.6 45.9 %all-gather.8.cloned.1.call-done = bf16[2,1024,384]{2,1,0:T(8,128)(2,1)} async-done(((bf16[2,32,384]{2,1,0:T(8,128)(2,1)}), bf16[2,1024,384]{2,1,0:T(8,128)(2,1)}) %all-gather.8.cloned.1.call-update) | async-done | bytes 1572880 | tf_op jit(solution)/shard_map/all_gather | solution.py:149
  331.5 2.6 fusion.126
  334.2 2.3 copy.180
  339.0 2.4 copy.181
  341.4 1.5 fusion.17
  342.9 1.5 fusion.29
  347.0 20.8 %reduce-scatter.5.cloned.1.call-done = bf16[768,32]{0,1:T(8,128)(2,1)} async-done(((bf16[3072,32]{0,1:T(8,128)(2,1)}), bf16[768,32]{0,1:T(8,128)(2,1)}) %reduce-scatter.5.cloned.1.call-update) | async-done | bytes 49168 | tf_op jit(solution)/shard_map/reduce_scatter | solution.py:176
  367.8 1.5 fusion.77
  (222 shorter events, 46.1 us)
Async XLA Ops:
  7.2 199.4 %copy-start = (bf16[1,384,3072]{2,1,0:T(8,128)(2,1)S(1)}, bf16[1,384,3072]{2,1,0:T(8,128)(2,1)}, u32[]{:S(2)}) copy-start(bf16[1,384,3072]{2,1,0:T(8,128)(2,1)} %param.12) | copy-start | bytes 7077892
  7.2 129.5 %all-gather.6.cloned.1.call-start = ((), (), s32[]{:S(2)}) async-start(), calls=%async_computation.2 | async-start | bytes 1622016 | tf_op jit(solution)/shard_map/all_gather | solution.py:149
  7.3 241.3 %copy-start.28 = (pred[32]{0:T(512)(128)(4,1)}, pred[32]{0:T(512)(128)(4,1)S(1)}, u32[]{:S(2)}) copy-start(pred[32]{0:T(512)(128)(4,1)S(1)} %fusion.119) | copy-start | bytes 100
  82.1 2.9 copy-start.34
  83.1 4.7 %copy-start.36 = (s32[4]{0:T(128)S(1)}, s32[4]{0:T(128)}, u32[]{:S(2)}) copy-start(s32[4]{0:T(128)} %param.15) | copy-start | bytes 52
  83.8 55.3 %copy-start.31 = (f32[64]{0:T(128)}, f32[64]{0:T(128)S(1)}, u32[]{:S(2)}) copy-start(f32[64]{0:T(128)S(1)} %get-tuple-element.47) | copy-start | bytes 772
  83.9 4.3 %copy-start.30 = (f32[384]{0:T(512)}, f32[384]{0:T(512)S(1)}, u32[]{:S(2)}) copy-start(f32[384]{0:T(512)S(1)} %mul.449) | copy-start | bytes 4612
  84.0 4.2 %copy-start.23 = (f32[384]{0:T(512)}, f32[384]{0:T(512)S(1)}, u32[]{:S(2)}) copy-start(f32[384]{0:T(512)S(1)} %mul.459) | copy-start | bytes 4612
  84.4 54.8 %copy-start.33 = (pred[384]{0:T(512)(128)(4,1)}, pred[384]{0:T(512)(128)(4,1)S(1)}, u32[]{:S(2)}) copy-start(pred[384]{0:T(512)(128)(4,1)S(1)} %fusion.111) | copy-start | bytes 1156
  85.3 3.1 copy-start.8
  85.4 3.1 copy-start.9
  85.5 3.0 copy-start.6
  85.6 2.9 copy-start.7
  86.4 103.3 %all-gather.10.cloned.1.call-start = ((), (), s32[]{:S(2)}) async-start(), calls=%async_computation.6 | async-start | bytes 1622016 | tf_op jit(solution)/shard_map/all_gather | solution.py:150
  87.1 142.1 %reduce-scatter.3.cloned.1.call-start = ((), (), s32[]{:S(2)}) async-start(), calls=%async_computation.3 | async-start | bytes 245760 | tf_op jit(solution)/shard_map/reduce_scatter | solution.py:176
  88.3 116.4 %copy-start.2 = (pred[32,1024]{1,0:T(8,128)(4,1)}, pred[32,1024]{1,0:T(8,128)(4,1)S(1)}, u32[]{:S(2)}) copy-start(pred[32,1024]{1,0:T(8,128)(4,1)S(1)} %broadcast_compare_fusion) | copy-start | bytes 98308
  204.7 24.6 %copy-start.16 = (bf16[32,768]{1,0:T(8,128)(2,1)S(1)}, bf16[32,768]{1,0:T(8,128)(2,1)}, u32[]{:S(2)}) copy-start(bf16[32,768]{1,0:T(8,128)(2,1)} %param.9) | copy-start | bytes 147460
  207.8 123.7 %all-gather.8.cloned.1.call-start = ((), (), s32[]{:S(2)}) async-start(), calls=%async_computation.4 | async-start | bytes 1622016 | tf_op jit(solution)/shard_map/all_gather | solution.py:149
  208.0 40.5 %copy-start.24 = (f32[768]{0:T(1024)}, f32[768]{0:T(1024)S(1)}, u32[]{:S(2)}) copy-start(f32[768]{0:T(1024)S(1)} %get-tuple-element.2) | copy-start | bytes 9220
  208.0 40.5 %copy-start.26 = (f32[768]{0:T(1024)}, f32[768]{0:T(1024)S(1)}, u32[]{:S(2)}) copy-start(f32[768]{0:T(1024)S(1)} %get-tuple-element.3) | copy-start | bytes 9220
  230.2 18.4 %copy-start.14 = (bf16[32,768]{1,0:T(8,128)(2,1)}, bf16[32,768]{1,0:T(8,128)(2,1)S(1)}, u32[]{:S(2)}) copy-start(bf16[32,768]{1,0:T(8,128)(2,1)S(1)} %fusion.65) | copy-start | bytes 147460
  230.2 5.2 %collective-permute-start = (bf16[32,768]{1,0:T(8,128)(2,1)S(1)}, bf16[32,768]{1,0:T(8,128)(2,1)S(1)}, u32[]{:S(2)}, u32[]{:S(2)}) collective-permute-start(bf16[32,768]{1,0:T(8,128)(2,1)S(1)} %fusion.65), channel_id=1, source_target_pairs={{0,128},{1,129},{2,130},{3,131},{4,132},{5,133},{6,134},{7,135},{8... | collective-permute-start | bytes 147464 | tf_op jit(solution)/shard_map/ppermute | solution.py:15
  279.6 88.2 %reduce-scatter.5.cloned.1.call-start = ((), (), s32[]{:S(2)}) async-start(), calls=%async_computation.5 | async-start | bytes 245760 | tf_op jit(solution)/shard_map/reduce_scatter | solution.py:176
  285.6 50.9 %copy-start.5 = (bf16[32,6,64]{2,0,1:T(8,128)(2,1)S(1)}, bf16[32,6,64]{2,0,1:T(8,128)(2,1)}, u32[]{:S(2)}) copy-start(bf16[32,6,64]{2,0,1:T(8,128)(2,1)} %fusion.71) | copy-start | bytes 73732
  334.2 3.7 copy-start.3
  339.0 3.8 %copy-start.1 = (f32[6,32,1024]{2,1,0:T(8,128)S(1)}, f32[6,32,1024]{2,1,0:T(8,128)}, u32[]{:S(2)}) copy-start(f32[6,32,1024]{2,1,0:T(8,128)} %get-tuple-element.54) | copy-start | bytes 2359300
  341.4 3.0 copy-start.4
  344.5 23.3 %copy-start.15 = (bf16[32,768]{1,0:T(8,128)(2,1)S(1)}, bf16[32,768]{1,0:T(8,128)(2,1)}, u32[]{:S(2)}) copy-start(bf16[32,768]{1,0:T(8,128)(2,1)} %copy-done.14) | copy-start | bytes 147460
  344.5 23.3 %copy-start.18 = (bf16[32,768]{1,0:T(8,128)(2,1)S(1)}, bf16[32,768]{1,0:T(8,128)(2,1)}, u32[]{:S(2)}) copy-start(bf16[32,768]{1,0:T(8,128)(2,1)} %copy-done.17) | copy-start | bytes 147460
  344.5 23.3 %copy-start.25 = (f32[768]{0:T(1024)S(1)}, f32[768]{0:T(1024)}, u32[]{:S(2)}) copy-start(f32[768]{0:T(1024)} %copy-done.24) | copy-start | bytes 9220
  344.5 23.3 %copy-start.27 = (f32[768]{0:T(1024)S(1)}, f32[768]{0:T(1024)}, u32[]{:S(2)}) copy-start(f32[768]{0:T(1024)} %copy-done.26) | copy-start | bytes 9220
  344.5 23.3 %copy-start.29 = (pred[32]{0:T(512)(128)(4,1)S(1)}, pred[32]{0:T(512)(128)(4,1)}, u32[]{:S(2)}) copy-start(pred[32]{0:T(512)(128)(4,1)} %copy-done.28) | copy-start | bytes 100
  (11 other events, 14.1 us)
Sparse Core Ops, SparseCore 0:
  86.5 50.1 all-gather.5
  139.3 50.2 all-gather.9
  208.0 21.2 reduce-scatter.2
  279.7 51.7 all-gather.7
  346.4 21.3 reduce-scatter.4
where the time goes:
time: 378 us; the launch traced here: 376 us
  waiting for transfers between devices  188 us (50%)
  blocking collectives  77.7 us (21%)
  local copies, waits for them, and re-layouts  47.8 us (13%)
  matrix products  23.4 us (6%)
  other arithmetic  19 us (5%)
  between operations  16.1 us (4%)
  starting transfers between devices  3.86 us (1%)
    all_gather x2, waiting for transfers between devices, attend(): lax.all_gather(fresh_kv, 'seq', axis=1, tiled=True)  94.1 us
    all_gather x1, waiting for transfers between devices, attend(): lax.all_gather(stale_own, 'seq', axis=1, tiled=True)  49.3 us
    all_gather x1, blocking collectives, local(): lax.all_gather(jnp.pad(by_tp.reshape(1, 4, -1), ((0, 0), (0, 4), (0, 0)))...  42.5 us
    reduce_scatter x2, waiting for transfers between devices, run_layer(): lax.psum_scatter(lax.dot_general(weights_out, attended, (((0,), (1,)), ((...  42 us
    all_gather x2, blocking collectives, run_layer(): lax.all_gather(incoming, 'tp', axis=1, tiled=True).astype(jnp.float32)  24.5 us
    unnamed x1, blocking collectives  10.7 us
    dot_general x2, matrix products, run_layer(): jnp.einsum('td,dcf->tcf', normed, weights_qkv, preferred_element_type=jnp...  8.79 us
    slice x4, local copies, waits for them, and re-layouts, merge_block(): fresh_keys = fresh_block[0].reshape(key_count, head_count, HEAD)  8.52 us
  transfers between devices with their start and end apart: 6, of which 6 were waited for; matrix products, arithmetic and copies ran while one was open for 3% of the time, Pallas kernels for 0%

commit v1 on v0

--- a/solution.py
+++ b/solution.py
@@ -7,6 +7,19 @@
 HEAD = 64
 TEMB = 512
 TEXT = 226
+
+
+def collect(array, axis, dim):
+    ways = lax.axis_size(axis)
+    up = [(d, (d + 1) % ways) for d in range(ways)]
+    down = [(d, (d - 1) % ways) for d in range(ways)]
+    earlier, later = ([array], [array])
+    for _ in range(ways // 2):
+        earlier.append(lax.ppermute(earlier[-1], axis, up))
+    for _ in range((ways - 1) // 2):
+        later.append(lax.ppermute(later[-1], axis, down))
+    line = jnp.concatenate([*earlier[::-1], *later[1:]], axis=dim)
+    return jnp.roll(line, (lax.axis_index(axis) - ways // 2) * array.shape[dim], axis=dim)
 
 
 def shifted(value, axis, steps):
@@ -154,7 +167,7 @@
         return jnp.transpose(blended, (1, 0, 2)).reshape(tok_rows, head_cols).astype(jnp.bfloat16)
 
     def run_layer(incoming):
-        features_all = lax.all_gather(incoming, "tp", axis=1, tiled=True).astype(jnp.float32)
+        features_all = collect(incoming, "tp", 1).astype(jnp.float32)
         average = jnp.mean(features_all, axis=1, keepdims=True)
         centred = features_all - average
         variance = jnp.mean(centred * centred, axis=1, keepdims=True)

time: 378 us -> 316 us (0.84)
  waiting for transfers between devices: 188 us -> 142 us
  blocking collectives: 77.7 us -> 52.2 us
  starting transfers between devices: 3.86 us -> 11.3 us
    all_gather x1, waiting for transfers between devices: 49.3 us -> 0.02 us  [attend(): lax.all_gather(stale_own, 'seq', axis=1, tiled=True)]
    all_gather x2 -> x0, blocking collectives: 24.5 us -> none  [run_layer(): lax.all_gather(incoming, 'tp', axis=1, tiled=True).astype(jnp.float32)]
    ppermute x0 -> x6, waiting for transfers between devices: none -> 11.5 us  [the longest x4 11.5 us: collect(): earlier.append(lax.ppermute(earlier[-1], axis, up))]
    ppermute x0 -> x6, starting transfers between devices: none -> 7.65 us  [the longest x2 4.89 us: collect(): later.append(lax.ppermute(later[-1], axis, down))]
    all_gather x2, waiting for transfers between devices: 94.1 us -> 86.5 us  [attend(): lax.all_gather(fresh_kv, 'seq', axis=1, tiled=True)]
  transfers between devices with their start and end apart: 6 -> 12, of which waited for: 6 -> 8; matrix products, arithmetic and copies ran while one was open for 3% -> 9% of each run, Pallas kernels for 0% -> 0%
where the time goes in v1:
time: 316 us; the launch traced here: 314 us
  waiting for transfers between devices  142 us (45%)
  blocking collectives  52.2 us (17%)
  local copies, waits for them, and re-layouts  49.4 us (16%)
  other arithmetic  21.9 us (7%)
  matrix products  21.4 us (7%)
  between operations  16 us (5%)
  starting transfers between devices  11.3 us (4%)
    all_gather x2, waiting for transfers between devices, attend(): lax.all_gather(fresh_kv, 'seq', axis=1, tiled=True)  86.5 us
    all_gather x1, blocking collectives, local(): lax.all_gather(jnp.pad(by_tp.reshape(1, 4, -1), ((0, 0), (0, 4), (0, 0)))...  42.6 us
    reduce_scatter x2, waiting for transfers between devices, run_layer(): lax.psum_scatter(lax.dot_general(weights_out, attended, (((0,), (1,)), ((...  42 us
    ppermute x4, waiting for transfers between devices, collect(): earlier.append(lax.ppermute(earlier[-1], axis, up))  11.5 us
    slice x4, local copies, waits for them, and re-layouts, merge_block(): fresh_keys = fresh_block[0].reshape(key_count, head_count, HEAD)  9.97 us
    unnamed x1, blocking collectives  9.51 us
    dot_general x2, matrix products, run_layer(): jnp.einsum('td,dcf->tcf', normed, weights_qkv, preferred_element_type=jnp...  8.79 us
    sub x10, local copies, waits for them, and re-layouts, head_norm(): centred = parts - average  7.57 us
  transfers between devices with their start and end apart: 12, of which 8 were waited for; matrix products, arithmetic and copies ran while one was open for 9% of the time, Pallas kernels for 0%

profile of v1, /device:TPU:2, one launch (start us, length us, event | category | flops | bytes accessed | tf_op | source)
XLA Modules:
  0.0 314.1 jit_solution(4986793873058801983)
XLA Ops:
  7.2 1.7 collective-permute-start
  8.9 1.7 collective-permute-start.2
  14.5 9.5 %all-reduce.1 = f32[576]{0:T(1024)S(1)} all-reduce(f32[576]{0:T(1024)S(1)} %dynamic-update-slice), channel_id=2, replica_groups=mesh['section'=2,'seq'=32,'tp'=4] {'tp'}, use_global_device_ids=true, to_apply=%add.1 | all-reduce | flops 576 | bytes 4608
  24.1 42.6 %all_gather.17 = f32[32,8,144]{2,1,0:T(8,128)S(1)} all-gather(f32[1,8,144]{2,1,0:T(8,128)S(1)} %pad.4), channel_id=1, replica_groups=mesh['section'=2,'seq'=32,'tp'=4] {'seq'}, dimensions={0}, use_global_device_ids=true | all-gather | bytes 152064 | tf_op jit(solution)/shard_map/all_gather | solution.py:134
  70.4 3.7 %collective-permute-done.1 = bf16[32,768]{1,0:T(8,128)(2,1)S(1)} collective-permute-done((bf16[32,768]{1,0:T(8,128)(2,1)S(1)}, bf16[32,768]{1,0:T(8,128)(2,1)S(1)}, u32[]{:S(2)}, u32[]{:S(2)}) %collective-permute-start.1) | collective-permute-done | bytes 49184 | tf_op jit(solution)/shard_map/ppermute | solution.py:18
  75.9 4.4 %fusion.2 = f32[32,3,384]{2,0,1:T(8,128)S(1)} fusion(bf16[1,3072,3,384]{3,1,2,0:T(8,128)(2,1)} %param.12, bf16[32,3072]{1,0:T(8,128)(2,1)S(1)} %get-tuple-element.8, f32[3072]{0:T(1024)S(1)} %bitcast.178, f32[3072]{0:T(1024)S(1)} %bitcast.180, f32[3072]{0:T(1024)S(1)} %bitcast.182, f32[3072]{0:T(1024)S(1)} %bitcast.176, f32[32]{0:T(128)S(1)} %add_rsqrt_fusion.5, ...), kind=kOutput, calls=%fused_computation.2 | convolution fusion | flops 227377152 | bytes 7471392 | tf_op jit(solution)/shard_map/td,dcf->tcf/dot_general | solution.py:177
  85.2 2.7 fusion.143
  89.3 2.3 copy.168
  91.6 41.6 %all-gather.6.cloned.1.call-done = bf16[2,1024,384]{2,1,0:T(8,128)(2,1)} async-done(((bf16[2,32,384]{2,1,0:T(8,128)(2,1)}), bf16[2,1024,384]{2,1,0:T(8,128)(2,1)}) %all-gather.6.cloned.1.call-update) | async-done | bytes 1572880 | tf_op jit(solution)/shard_map/all_gather | solution.py:162
  133.2 2.7 fusion.144
  135.9 2.3 copy.165
  140.7 2.3 copy.167
  143.0 1.5 fusion.16
  144.5 1.8 fusion.28
  148.3 21.3 %reduce-scatter.3.cloned.1.call-done = bf16[768,32]{0,1:T(8,128)(2,1)} async-done(((bf16[3072,32]{0,1:T(8,128)(2,1)}), bf16[768,32]{0,1:T(8,128)(2,1)}) %reduce-scatter.3.cloned.1.call-update) | async-done | bytes 49168 | tf_op jit(solution)/shard_map/reduce_scatter | solution.py:189
  170.5 3.5 %collective-permute-start.3 = (bf16[32,768]{1,0:T(8,128)(2,1)S(1)}, bf16[32,768]{1,0:T(8,128)(2,1)S(1)}, u32[]{:S(2)}, u32[]{:S(2)}) collective-permute-start(bf16[32,768]{1,0:T(8,128)(2,1)S(1)} %fusion.79), channel_id=1, source_target_pairs={{0,128},{1,129},{2,130},{3,131},{4,132},{5,133},{6,134},{7,135},{8... | collective-permute-start | bytes 147464 | tf_op jit(solution)/shard_map/ppermute | solution.py:28
  174.0 1.7 collective-permute-done.3
  175.7 3.2 %collective-permute-start.6 = (bf16[32,768]{1,0:T(8,128)(2,1)S(1)}, bf16[32,768]{1,0:T(8,128)(2,1)S(1)}, u32[]{:S(2)}, u32[]{:S(2)}) collective-permute-start(bf16[32,768]{1,0:T(8,128)(2,1)S(1)} %collective-permute-done.3), channel_id=1, source_target_pairs={{0,3},{1,0},{2,1},{3,2},{4,7},{5,4},{6,5},{7,6},{8,11},{9,8},{10,9... | collective-permute-start | bytes 147464 | tf_op jit(solution)/shard_map/ppermute | solution.py:20
  179.0 2.5 collective-permute-done.4
  181.5 5.3 %collective-permute-done.5 = bf16[32,768]{1,0:T(8,128)(2,1)S(1)} collective-permute-done((bf16[32,768]{1,0:T(8,128)(2,1)S(1)}, bf16[32,768]{1,0:T(8,128)(2,1)S(1)}, u32[]{:S(2)}, u32[]{:S(2)}) %collective-permute-start.5) | collective-permute-done | bytes 49184 | tf_op jit(solution)/shard_map/ppermute | solution.py:18
  187.9 4.4 %fusion = f32[32,3,384]{2,0,1:T(8,128)S(1)} fusion(bf16[1,3072,3,384]{3,1,2,0:T(8,128)(2,1)} %param.12, bf16[32,3072]{1,0:T(8,128)(2,1)S(1)} %get-tuple-element.6, f32[32]{0:T(128)S(1)} %add_rsqrt_fusion.4, f32[32]{0:T(128)S(1)} %broadcast_multiply_fusion.7, f32[3072]{0:T(1024)S(1)} %bitcast.179, f32[3072]{0:T(1024)S(1)} %bitcast.181, f32[3072]{0:T(1024)S(1)} %bitcast.183, ...), kind=kOutput, calls=%fused_computation | convolution fusion | flops 227377152 | bytes 7471392 | tf_op jit(solution)/shard_map/td,dcf->tcf/dot_general | solution.py:177
  203.7 1.6 mul.484
  206.8 1.6 sub.171
  209.9 1.6 sub.177
  211.5 1.5 fusion.107
  224.8 44.9 %all-gather.8.cloned.1.call-done = bf16[2,1024,384]{2,1,0:T(8,128)(2,1)} async-done(((bf16[2,32,384]{2,1,0:T(8,128)(2,1)}), bf16[2,1024,384]{2,1,0:T(8,128)(2,1)}) %all-gather.8.cloned.1.call-update) | async-done | bytes 1572880 | tf_op jit(solution)/shard_map/all_gather | solution.py:162
  269.7 2.7 fusion.142
  272.4 2.3 copy.180
  277.3 2.4 copy.181
  281.1 1.5 fusion.29
  285.2 20.8 %reduce-scatter.5.cloned.1.call-done = bf16[768,32]{0,1:T(8,128)(2,1)} async-done(((bf16[3072,32]{0,1:T(8,128)(2,1)}), bf16[768,32]{0,1:T(8,128)(2,1)}) %reduce-scatter.5.cloned.1.call-update) | async-done | bytes 49168 | tf_op jit(solution)/shard_map/reduce_scatter | solution.py:189
  306.0 1.5 fusion.91
  (232 shorter events, 53.1 us)
Async XLA Ops:
  7.2 139.7 %copy-start = (bf16[1,384,3072]{2,1,0:T(8,128)(2,1)S(1)}, bf16[1,384,3072]{2,1,0:T(8,128)(2,1)}, u32[]{:S(2)}) copy-start(bf16[1,384,3072]{2,1,0:T(8,128)(2,1)} %param.14) | copy-start | bytes 7077892
  7.2 78.0 %all-gather.10.cloned.1.call-start = ((), (), s32[]{:S(2)}) async-start(), calls=%async_computation.6 | async-start | bytes 1622016 | tf_op jit(solution)/shard_map/all_gather | solution.py:163
  7.2 61.5 %collective-permute-start = (bf16[32,768]{1,0:T(8,128)(2,1)}, bf16[32,768]{1,0:T(8,128)(2,1)S(1)}, u32[]{:S(2)}, u32[]{:S(2)}) collective-permute-start(bf16[32,768]{1,0:T(8,128)(2,1)} %param.11), channel_id=1, source_target_pairs={{0,1},{1,2},{2,3},{3,0},{4,5},{5,6},{6,7},{7,4},{8,9},{9,10},{10,1... | collective-permute-start | bytes 147464 | tf_op jit(solution)/shard_map/ppermute | solution.py:18
  8.9 61.5 %collective-permute-start.2 = (bf16[32,768]{1,0:T(8,128)(2,1)}, bf16[32,768]{1,0:T(8,128)(2,1)S(1)}, u32[]{:S(2)}, u32[]{:S(2)}) collective-permute-start(bf16[32,768]{1,0:T(8,128)(2,1)} %param.11), channel_id=1, source_target_pairs={{0,3},{1,0},{2,1},{3,2},{4,7},{5,4},{6,5},{7,6},{8,11},{9,8},{10,9... | collective-permute-start | bytes 147464 | tf_op jit(solution)/shard_map/ppermute | solution.py:20
  10.6 122.6 %all-gather.6.cloned.1.call-start = ((), (), s32[]{:S(2)}) async-start(), calls=%async_computation.2 | async-start | bytes 1622016 | tf_op jit(solution)/shard_map/all_gather | solution.py:162
  67.8 17.2 %copy-start.33 = (f32[64]{0:T(128)}, f32[64]{0:T(128)S(1)}, u32[]{:S(2)}) copy-start(f32[64]{0:T(128)S(1)} %get-tuple-element.52) | copy-start | bytes 772
  68.7 14.3 %copy-start.35 = (pred[384]{0:T(512)(128)(4,1)}, pred[384]{0:T(512)(128)(4,1)S(1)}, u32[]{:S(2)}) copy-start(pred[384]{0:T(512)(128)(4,1)S(1)} %fusion.125) | copy-start | bytes 1156
  68.8 5.4 %collective-permute-start.1 = (bf16[32,768]{1,0:T(8,128)(2,1)S(1)}, bf16[32,768]{1,0:T(8,128)(2,1)S(1)}, u32[]{:S(2)}, u32[]{:S(2)}) collective-permute-start(bf16[32,768]{1,0:T(8,128)(2,1)S(1)} %collective-permute-done), channel_id=1, source_target_pairs={{0,1},{1,2},{2,3},{3,0},{4,5},{5,6},{6,7},{7,4},{8,9},{9,10},{10,1... | collective-permute-start | bytes 147464 | tf_op jit(solution)/shard_map/ppermute | solution.py:18
  69.9 118.0 %copy-start.30 = (pred[32]{0:T(512)(128)(4,1)}, pred[32]{0:T(512)(128)(4,1)S(1)}, u32[]{:S(2)}) copy-start(pred[32]{0:T(512)(128)(4,1)S(1)} %fusion.133) | copy-start | bytes 100
  70.0 13.0 %copy-start.25 = (f32[384]{0:T(512)}, f32[384]{0:T(512)S(1)}, u32[]{:S(2)}) copy-start(f32[384]{0:T(512)S(1)} %mul.464) | copy-start | bytes 4612
  70.1 14.9 %copy-start.10 = (f32[32,64]{1,0:T(8,128)}, f32[32,64]{1,0:T(8,128)S(1)}, u32[]{:S(2)}) copy-start(f32[32,64]{1,0:T(8,128)S(1)} %copy.155) | copy-start | bytes 24580
  70.2 14.8 %copy-start.11 = (f32[32,64]{1,0:T(8,128)}, f32[32,64]{1,0:T(8,128)S(1)}, u32[]{:S(2)}) copy-start(f32[32,64]{1,0:T(8,128)S(1)} %copy.160) | copy-start | bytes 24580
  70.3 12.7 %copy-start.8 = (f32[1,32,384]{2,1,0:T(8,128)}, f32[1,32,384]{2,1,0:T(8,128)S(1)}, u32[]{:S(2)}) copy-start(f32[1,32,384]{2,1,0:T(8,128)S(1)} %tile.20) | copy-start | bytes 147460
  70.4 12.6 %copy-start.9 = (f32[1,32,384]{2,1,0:T(8,128)}, f32[1,32,384]{2,1,0:T(8,128)S(1)}, u32[]{:S(2)}) copy-start(f32[1,32,384]{2,1,0:T(8,128)S(1)} %tile.21) | copy-start | bytes 147460
  83.8 85.8 %reduce-scatter.3.cloned.1.call-start = ((), (), s32[]{:S(2)}) async-start(), calls=%async_computation.3 | async-start | bytes 245760 | tf_op jit(solution)/shard_map/reduce_scatter | solution.py:189
  84.4 61.9 %copy-start.3 = (pred[32,1024]{1,0:T(8,128)(4,1)}, pred[32,1024]{1,0:T(8,128)(4,1)S(1)}, u32[]{:S(2)}) copy-start(pred[32,1024]{1,0:T(8,128)(4,1)S(1)} %broadcast_compare_fusion) | copy-start | bytes 98308
  146.3 23.3 %copy-start.16 = (bf16[32,768]{1,0:T(8,128)(2,1)S(1)}, bf16[32,768]{1,0:T(8,128)(2,1)}, u32[]{:S(2)}) copy-start(bf16[32,768]{1,0:T(8,128)(2,1)} %param.11) | copy-start | bytes 147460
  148.1 121.6 %all-gather.8.cloned.1.call-start = ((), (), s32[]{:S(2)}) async-start(), calls=%async_computation.4 | async-start | bytes 1622016 | tf_op jit(solution)/shard_map/all_gather | solution.py:162
  148.3 25.7 %copy-start.26 = (f32[768]{0:T(1024)}, f32[768]{0:T(1024)S(1)}, u32[]{:S(2)}) copy-start(f32[768]{0:T(1024)S(1)} %get-tuple-element.3) | copy-start | bytes 9220
  148.3 25.7 %copy-start.28 = (f32[768]{0:T(1024)}, f32[768]{0:T(1024)S(1)}, u32[]{:S(2)}) copy-start(f32[768]{0:T(1024)S(1)} %get-tuple-element.4) | copy-start | bytes 9220
  170.5 21.8 %copy-start.17 = (bf16[32,768]{1,0:T(8,128)(2,1)}, bf16[32,768]{1,0:T(8,128)(2,1)S(1)}, u32[]{:S(2)}) copy-start(bf16[32,768]{1,0:T(8,128)(2,1)S(1)} %fusion.79) | copy-start | bytes 147460
  170.5 5.2 %collective-permute-start.3 = (bf16[32,768]{1,0:T(8,128)(2,1)S(1)}, bf16[32,768]{1,0:T(8,128)(2,1)S(1)}, u32[]{:S(2)}, u32[]{:S(2)}) collective-permute-start(bf16[32,768]{1,0:T(8,128)(2,1)S(1)} %fusion.79), channel_id=1, source_target_pairs={{0,128},{1,129},{2,130},{3,131},{4,132},{5,133},{6,134},{7,135},{8... | collective-permute-start | bytes 147464 | tf_op jit(solution)/shard_map/ppermute | solution.py:28
  175.7 5.7 %collective-permute-start.4 = (bf16[32,768]{1,0:T(8,128)(2,1)S(1)}, bf16[32,768]{1,0:T(8,128)(2,1)S(1)}, u32[]{:S(2)}, u32[]{:S(2)}) collective-permute-start(bf16[32,768]{1,0:T(8,128)(2,1)S(1)} %collective-permute-done.3), channel_id=1, source_target_pairs={{0,1},{1,2},{2,3},{3,0},{4,5},{5,6},{6,7},{7,4},{8,9},{9,10},{10,1... | collective-permute-start | bytes 147464 | tf_op jit(solution)/shard_map/ppermute | solution.py:18
  175.7 5.7 %collective-permute-start.6 = (bf16[32,768]{1,0:T(8,128)(2,1)S(1)}, bf16[32,768]{1,0:T(8,128)(2,1)S(1)}, u32[]{:S(2)}, u32[]{:S(2)}) collective-permute-start(bf16[32,768]{1,0:T(8,128)(2,1)S(1)} %collective-permute-done.3), channel_id=1, source_target_pairs={{0,3},{1,0},{2,1},{3,2},{4,7},{5,4},{6,5},{7,6},{8,11},{9,8},{10,9... | collective-permute-start | bytes 147464 | tf_op jit(solution)/shard_map/ppermute | solution.py:20
  181.5 5.3 %collective-permute-start.5 = (bf16[32,768]{1,0:T(8,128)(2,1)S(1)}, bf16[32,768]{1,0:T(8,128)(2,1)S(1)}, u32[]{:S(2)}, u32[]{:S(2)}) collective-permute-start(bf16[32,768]{1,0:T(8,128)(2,1)S(1)} %collective-permute-done.4), channel_id=1, source_target_pairs={{0,1},{1,2},{2,3},{3,0},{4,5},{5,6},{6,7},{7,4},{8,9},{9,10},{10,1... | collective-permute-start | bytes 147464 | tf_op jit(solution)/shard_map/ppermute | solution.py:18
  218.9 87.1 %reduce-scatter.5.cloned.1.call-start = ((), (), s32[]{:S(2)}) async-start(), calls=%async_computation.5 | async-start | bytes 245760 | tf_op jit(solution)/shard_map/reduce_scatter | solution.py:189
  224.8 49.9 %copy-start.7 = (bf16[32,6,64]{2,0,1:T(8,128)(2,1)S(1)}, bf16[32,6,64]{2,0,1:T(8,128)(2,1)}, u32[]{:S(2)}) copy-start(bf16[32,6,64]{2,0,1:T(8,128)(2,1)} %fusion.85) | copy-start | bytes 73732
  282.7 23.3 %copy-start.18 = (bf16[32,768]{1,0:T(8,128)(2,1)S(1)}, bf16[32,768]{1,0:T(8,128)(2,1)}, u32[]{:S(2)}) copy-start(bf16[32,768]{1,0:T(8,128)(2,1)} %copy-done.17) | copy-start | bytes 147460
  282.7 23.3 %copy-start.20 = (bf16[32,768]{1,0:T(8,128)(2,1)S(1)}, bf16[32,768]{1,0:T(8,128)(2,1)}, u32[]{:S(2)}) copy-start(bf16[32,768]{1,0:T(8,128)(2,1)} %copy-done.19) | copy-start | bytes 147460
  282.7 23.3 %copy-start.27 = (f32[768]{0:T(1024)S(1)}, f32[768]{0:T(1024)}, u32[]{:S(2)}) copy-start(f32[768]{0:T(1024)} %copy-done.26) | copy-start | bytes 9220
  282.8 23.3 %copy-start.29 = (f32[768]{0:T(1024)S(1)}, f32[768]{0:T(1024)}, u32[]{:S(2)}) copy-start(f32[768]{0:T(1024)} %copy-done.28) | copy-start | bytes 9220
  282.8 23.2 %copy-start.31 = (pred[32]{0:T(512)(128)(4,1)S(1)}, pred[32]{0:T(512)(128)(4,1)}, u32[]{:S(2)}) copy-start(pred[32]{0:T(512)(128)(4,1)} %copy-done.30) | copy-start | bytes 100
  (17 other events, 61.3 us)
Sparse Core Ops, SparseCore 0:
  10.7 54.9 all-gather.9
  83.9 49.1 all-gather.5
  148.3 21.2 reduce-scatter.2
  219.1 50.6 all-gather.7
  284.7 21.2 reduce-scatter.4
